TPU v7x, 32 devices: a whole 2x2x4 slice. The times are simulated.
32 devices in a mesh: pairs: 16 (over z, y, core), aux: 2 (over x).
Axes of the slice: x: 2, y: 2, z: 4, core: 2. Of those that a mesh axis runs over, the one named last changes fastest.
Arguments:
- amplitudes: float32 [64, 256, 256], P('pairs'), may hold values from -6 to 6
- factors: float32 [384, 256, 256], P('aux', 'pairs'), may hold values from -0.078125 to 0.078125
- occ_factors: float32 [384, 8, 8], P('aux'), may hold values from -0.5 to 0.5
Outputs:
- resid: float32 [64, 256, 256], P(None, 'pairs', 'aux')
All inputs are finite; a program needn't handle non-finite values.
Results may differ from a plain program's by a relative error of at most 0.0001.
Values sent between devices are 32-bit elements; how exact they have to be, the bound alone decides.
No kernel may reach another device: no remote copies, remote signals or barrier semaphores. Data moves between devices by JAX's collectives and lax.ppermute only.
A program may use at most 128 MiB of HBM per device.

v0:
```python
import jax
import jax.numpy as jnp
from jax import lax
from jax.sharding import PartitionSpec as P

highest = lax.Precision.HIGHEST


def from_partner(value, axis, bit):
    mask = 2**bit
    pairs = [(source, source ^ mask) for source in range(lax.axis_size(axis))]
    return lax.ppermute(value, axis, pairs)


def both_sides(running, amps, row_block):
    mixed_terms = jnp.einsum("icd,pbd->picb", amps, row_block, precision=highest)
    return running + jnp.einsum("pac,picb->iab", row_block, mixed_terms, precision=highest)


def shards(amplitudes, factors, occ_factors):
    virt_width = amplitudes.shape[1]
    aux_local = factors.shape[0]
    local_rows = factors.shape[1]
    occupied = occ_factors.shape[1]
    total_pairs = occupied * occupied
    aux_rank = lax.axis_index("aux")
    column_count = virt_width // lax.axis_size("aux")
    col_start = aux_rank * column_count
    amp_cols = lax.dynamic_slice_in_dim(amplitudes, col_start, column_count, 2)
    amp_flip = jnp.swapaxes(lax.dynamic_slice_in_dim(amplitudes, col_start, column_count, 1), 1, 2)
    pairs_rank = lax.axis_index("pairs")
    pairs_count = lax.axis_size("pairs")
    quarter_rows = aux_local // 4
    quarters = factors.reshape(1, 4, quarter_rows, local_rows, virt_width)
    outgoing = jnp.tile(quarters, (pairs_count // 4, 1, 1, 1, 1)).reshape(
        pairs_count, quarter_rows, local_rows, virt_width
    )
    arrived = lax.all_to_all(outgoing, "pairs", split_axis=0, concat_axis=2, tiled=True)[0]
    group_amps = amplitudes
    for bit in range(2):
        mate = from_partner(group_amps, "pairs", bit)
        lower = pairs_rank // 2**bit % 2 == 0
        group_amps = jnp.where(
            lower, jnp.concatenate([group_amps, mate], 0), jnp.concatenate([mate, group_amps], 0)
        )

    def quarter_step(running, block_index):
        row_block = lax.dynamic_slice_in_dim(arrived, block_index * 2, 2, 0)
        return (both_sides(running, group_amps, row_block), None)

    group_part, unused = lax.scan(
        quarter_step, jnp.zeros(group_amps.shape, jnp.float32), jnp.arange(quarter_rows // 2)
    )
    for bit in (1, 0):
        half = group_part.shape[0] // 2
        lower = pairs_rank // 2**bit % 2 == 0
        keep = jnp.where(lower, group_part[:half], group_part[half:])
        sending = jnp.where(lower, group_part[half:], group_part[:half])
        group_part = keep + from_partner(sending, "pairs", bit)
    particle = group_part
    coupling = jnp.einsum("pik,pjl->ijkl", occ_factors, occ_factors, precision=highest).reshape(
        total_pairs, total_pairs
    )
    particle, coupling = lax.psum((particle, coupling), "aux")
    part_cols = lax.dynamic_slice_in_dim(particle, col_start, column_count, 2)
    part_flip = jnp.swapaxes(lax.dynamic_slice_in_dim(particle, col_start, column_count, 1), 1, 2)
    part_cols, part_flip, amp_cols, amp_flip = (
        lax.all_to_all(part_cols, "pairs", split_axis=1, concat_axis=0, tiled=True),
        lax.all_to_all(part_flip, "pairs", split_axis=1, concat_axis=0, tiled=True),
        lax.all_to_all(amp_cols, "pairs", split_axis=1, concat_axis=0, tiled=True),
        lax.all_to_all(amp_flip, "pairs", split_axis=1, concat_axis=0, tiled=True),
    )
    straight = part_cols + jnp.einsum("pk,kab->pab", coupling, amp_cols, precision=highest)
    turned = part_flip + jnp.einsum("pk,kab->pab", coupling, amp_flip, precision=highest)
    rows_here = turned.shape[1]
    turned = (
        turned.reshape(occupied, occupied, rows_here, column_count)
        .transpose(1, 0, 2, 3)
        .reshape(total_pairs, rows_here, column_count)
    )
    return straight + turned


def solution(mesh):
    placed = (P("pairs", None, None), P("aux", "pairs", None), P("aux", None, None))
    return jax.shard_map(
        shards, mesh=mesh, in_specs=placed, out_specs=P(None, "pairs", "aux"), check_vma=False
    )
```

profile of v0, /device:TPU:0, one launch (start us, length us, event | category | flops | bytes accessed | tf_op | source)
XLA Modules:
  0.0 1026.3 jit_solution(16674948247421829473)
XLA Ops:
  30.0 141.6 %collective-permute-done.1 = f32[8,256,256]{2,1,0:T(8,128)} collective-permute-done((f32[8,256,256]{2,1,0:T(8,128)S(1)}, f32[8,256,256]{2,1,0:T(8,128)}, u32[]{:S(2)}, u32[]{:S(2)}) %collective-permute-start.1) | collective-permute-done | bytes 2097184 | tf_op jit(solution)/shard_map/ppermute | solution.py:12
  176.3 69.7 %all-to-all-done = f32[16,48,16,256]{3,2,1,0:T(8,128)} async-done(((f32[16,48,16,256]{3,2,1,0:T(8,128)}), f32[16,48,16,256]{3,2,1,0:T(8,128)}, u32[]{:S(2)}, u32[]{:S(2)}) %all-to-all-start) | async-done | bytes 12582944 | tf_op jit(solution)/shard_map/all_to_all | solution.py:38
  246.0 11.4 %copy.49 = f32[16,48,16,256]{3,2,0,1:T(8,128)} copy(f32[16,48,16,256]{3,2,1,0:T(8,128)} %all-to-all-done) | data formatting | bytes 25165824 | tf_op jit(solution)/shard_map/all_to_all | solution.py:38
  257.3 560.0 %while.11 = (s32[]{:T(128)}, f32[16,256,256]{1,2,0:T(8,128)}, s32[24]{0:T(128)S(1)}, f32[48,256,256]{2,1,0:T(8,128)}, f32[16,256,256]{2,1,0:T(8,128)}, /*index=5*/s32[]{:T(128)}, s32[1]{0:T(128)}, s32[]{:T(128)}, s32[]{:T(128)}) while((s32[]{:T(128)}, f32[16,256,256]{1,2,0:T(8,128)}, s32[24]{0:T(128)S(1)}, ...), condition=%wide.region_1.2_spmd.clone, body=%wide.region_0.1_spmd.clone.sunk | while | flops 12886999040 | bytes 30408872 | solution.py:51
  292.2 11.3 %bitcast_add_fusion.2 = f32[16,256,256]{1,2,0:T(8,128)} fusion(f32[16,256,256]{1,2,0:T(8,128)} %get-tuple-element.102, f32[2,256,16,256]{3,1,0,2:T(8,128)} %fusion.29, pred[]{:T(512)S(6)} %compare.8, f32[48,256,256]{2,1,0:T(8,128)} %get-tuple-element.113, s32[]{:T(128)S(6)} %select_n.97), kind=kOutput, calls=%fused_computation.2.clone.1 | convolution fusion | flops 6444548096 | bytes 17301508 | tf_op jit(solution)/shard_map/while/body/eval_jaxpr/pac,picb->iab/dot_general | solution.py:17
  315.6 11.2 %bitcast_add_fusion.2 = f32[16,256,256]{1,2,0:T(8,128)} fusion(f32[16,256,256]{1,2,0:T(8,128)} %get-tuple-element.102, f32[2,256,16,256]{3,1,0,2:T(8,128)} %fusion.29, pred[]{:T(512)S(6)} %compare.8, f32[48,256,256]{2,1,0:T(8,128)} %get-tuple-element.113, s32[]{:T(128)S(6)} %select_n.97), kind=kOutput, calls=%fused_computation.2.clone.1 | convolution fusion | flops 6444548096 | bytes 17301508 | tf_op jit(solution)/shard_map/while/body/eval_jaxpr/pac,picb->iab/dot_general | solution.py:17
  338.9 11.2 %bitcast_add_fusion.2 = f32[16,256,256]{1,2,0:T(8,128)} fusion(f32[16,256,256]{1,2,0:T(8,128)} %get-tuple-element.102, f32[2,256,16,256]{3,1,0,2:T(8,128)} %fusion.29, pred[]{:T(512)S(6)} %compare.8, f32[48,256,256]{2,1,0:T(8,128)} %get-tuple-element.113, s32[]{:T(128)S(6)} %select_n.97), kind=kOutput, calls=%fused_computation.2.clone.1 | convolution fusion | flops 6444548096 | bytes 17301508 | tf_op jit(solution)/shard_map/while/body/eval_jaxpr/pac,picb->iab/dot_general | solution.py:17
  362.3 11.2 %bitcast_add_fusion.2 = f32[16,256,256]{1,2,0:T(8,128)} fusion(f32[16,256,256]{1,2,0:T(8,128)} %get-tuple-element.102, f32[2,256,16,256]{3,1,0,2:T(8,128)} %fusion.29, pred[]{:T(512)S(6)} %compare.8, f32[48,256,256]{2,1,0:T(8,128)} %get-tuple-element.113, s32[]{:T(128)S(6)} %select_n.97), kind=kOutput, calls=%fused_computation.2.clone.1 | convolution fusion | flops 6444548096 | bytes 17301508 | tf_op jit(solution)/shard_map/while/body/eval_jaxpr/pac,picb->iab/dot_general | solution.py:17
  385.6 11.2 %bitcast_add_fusion.2 = f32[16,256,256]{1,2,0:T(8,128)} fusion(f32[16,256,256]{1,2,0:T(8,128)} %get-tuple-element.102, f32[2,256,16,256]{3,1,0,2:T(8,128)} %fusion.29, pred[]{:T(512)S(6)} %compare.8, f32[48,256,256]{2,1,0:T(8,128)} %get-tuple-element.113, s32[]{:T(128)S(6)} %select_n.97), kind=kOutput, calls=%fused_computation.2.clone.1 | convolution fusion | flops 6444548096 | bytes 17301508 | tf_op jit(solution)/shard_map/while/body/eval_jaxpr/pac,picb->iab/dot_general | solution.py:17
  409.0 11.2 %bitcast_add_fusion.2 = f32[16,256,256]{1,2,0:T(8,128)} fusion(f32[16,256,256]{1,2,0:T(8,128)} %get-tuple-element.102, f32[2,256,16,256]{3,1,0,2:T(8,128)} %fusion.29, pred[]{:T(512)S(6)} %compare.8, f32[48,256,256]{2,1,0:T(8,128)} %get-tuple-element.113, s32[]{:T(128)S(6)} %select_n.97), kind=kOutput, calls=%fused_computation.2.clone.1 | convolution fusion | flops 6444548096 | bytes 17301508 | tf_op jit(solution)/shard_map/while/body/eval_jaxpr/pac,picb->iab/dot_general | solution.py:17
  432.3 11.2 %bitcast_add_fusion.2 = f32[16,256,256]{1,2,0:T(8,128)} fusion(f32[16,256,256]{1,2,0:T(8,128)} %get-tuple-element.102, f32[2,256,16,256]{3,1,0,2:T(8,128)} %fusion.29, pred[]{:T(512)S(6)} %compare.8, f32[48,256,256]{2,1,0:T(8,128)} %get-tuple-element.113, s32[]{:T(128)S(6)} %select_n.97), kind=kOutput, calls=%fused_computation.2.clone.1 | convolution fusion | flops 6444548096 | bytes 17301508 | tf_op jit(solution)/shard_map/while/body/eval_jaxpr/pac,picb->iab/dot_general | solution.py:17
  455.7 11.2 %bitcast_add_fusion.2 = f32[16,256,256]{1,2,0:T(8,128)} fusion(f32[16,256,256]{1,2,0:T(8,128)} %get-tuple-element.102, f32[2,256,16,256]{3,1,0,2:T(8,128)} %fusion.29, pred[]{:T(512)S(6)} %compare.8, f32[48,256,256]{2,1,0:T(8,128)} %get-tuple-element.113, s32[]{:T(128)S(6)} %select_n.97), kind=kOutput, calls=%fused_computation.2.clone.1 | convolution fusion | flops 6444548096 | bytes 17301508 | tf_op jit(solution)/shard_map/while/body/eval_jaxpr/pac,picb->iab/dot_general | solution.py:17
  479.0 11.2 %bitcast_add_fusion.2 = f32[16,256,256]{1,2,0:T(8,128)} fusion(f32[16,256,256]{1,2,0:T(8,128)} %get-tuple-element.102, f32[2,256,16,256]{3,1,0,2:T(8,128)} %fusion.29, pred[]{:T(512)S(6)} %compare.8, f32[48,256,256]{2,1,0:T(8,128)} %get-tuple-element.113, s32[]{:T(128)S(6)} %select_n.97), kind=kOutput, calls=%fused_computation.2.clone.1 | convolution fusion | flops 6444548096 | bytes 17301508 | tf_op jit(solution)/shard_map/while/body/eval_jaxpr/pac,picb->iab/dot_general | solution.py:17
  502.4 11.2 %bitcast_add_fusion.2 = f32[16,256,256]{1,2,0:T(8,128)} fusion(f32[16,256,256]{1,2,0:T(8,128)} %get-tuple-element.102, f32[2,256,16,256]{3,1,0,2:T(8,128)} %fusion.29, pred[]{:T(512)S(6)} %compare.8, f32[48,256,256]{2,1,0:T(8,128)} %get-tuple-element.113, s32[]{:T(128)S(6)} %select_n.97), kind=kOutput, calls=%fused_computation.2.clone.1 | convolution fusion | flops 6444548096 | bytes 17301508 | tf_op jit(solution)/shard_map/while/body/eval_jaxpr/pac,picb->iab/dot_general | solution.py:17
  525.7 11.3 %bitcast_add_fusion.2 = f32[16,256,256]{1,2,0:T(8,128)} fusion(f32[16,256,256]{1,2,0:T(8,128)} %get-tuple-element.102, f32[2,256,16,256]{3,1,0,2:T(8,128)} %fusion.29, pred[]{:T(512)S(6)} %compare.8, f32[48,256,256]{2,1,0:T(8,128)} %get-tuple-element.113, s32[]{:T(128)S(6)} %select_n.97), kind=kOutput, calls=%fused_computation.2.clone.1 | convolution fusion | flops 6444548096 | bytes 17301508 | tf_op jit(solution)/shard_map/while/body/eval_jaxpr/pac,picb->iab/dot_general | solution.py:17
  549.1 11.2 %bitcast_add_fusion.2 = f32[16,256,256]{1,2,0:T(8,128)} fusion(f32[16,256,256]{1,2,0:T(8,128)} %get-tuple-element.102, f32[2,256,16,256]{3,1,0,2:T(8,128)} %fusion.29, pred[]{:T(512)S(6)} %compare.8, f32[48,256,256]{2,1,0:T(8,128)} %get-tuple-element.113, s32[]{:T(128)S(6)} %select_n.97), kind=kOutput, calls=%fused_computation.2.clone.1 | convolution fusion | flops 6444548096 | bytes 17301508 | tf_op jit(solution)/shard_map/while/body/eval_jaxpr/pac,picb->iab/dot_general | solution.py:17
  572.5 11.2 %bitcast_add_fusion.2 = f32[16,256,256]{1,2,0:T(8,128)} fusion(f32[16,256,256]{1,2,0:T(8,128)} %get-tuple-element.102, f32[2,256,16,256]{3,1,0,2:T(8,128)} %fusion.29, pred[]{:T(512)S(6)} %compare.8, f32[48,256,256]{2,1,0:T(8,128)} %get-tuple-element.113, s32[]{:T(128)S(6)} %select_n.97), kind=kOutput, calls=%fused_computation.2.clone.1 | convolution fusion | flops 6444548096 | bytes 17301508 | tf_op jit(solution)/shard_map/while/body/eval_jaxpr/pac,picb->iab/dot_general | solution.py:17
  595.8 11.2 %bitcast_add_fusion.2 = f32[16,256,256]{1,2,0:T(8,128)} fusion(f32[16,256,256]{1,2,0:T(8,128)} %get-tuple-element.102, f32[2,256,16,256]{3,1,0,2:T(8,128)} %fusion.29, pred[]{:T(512)S(6)} %compare.8, f32[48,256,256]{2,1,0:T(8,128)} %get-tuple-element.113, s32[]{:T(128)S(6)} %select_n.97), kind=kOutput, calls=%fused_computation.2.clone.1 | convolution fusion | flops 6444548096 | bytes 17301508 | tf_op jit(solution)/shard_map/while/body/eval_jaxpr/pac,picb->iab/dot_general | solution.py:17
  619.2 11.3 %bitcast_add_fusion.2 = f32[16,256,256]{1,2,0:T(8,128)} fusion(f32[16,256,256]{1,2,0:T(8,128)} %get-tuple-element.102, f32[2,256,16,256]{3,1,0,2:T(8,128)} %fusion.29, pred[]{:T(512)S(6)} %compare.8, f32[48,256,256]{2,1,0:T(8,128)} %get-tuple-element.113, s32[]{:T(128)S(6)} %select_n.97), kind=kOutput, calls=%fused_computation.2.clone.1 | convolution fusion | flops 6444548096 | bytes 17301508 | tf_op jit(solution)/shard_map/while/body/eval_jaxpr/pac,picb->iab/dot_general | solution.py:17
  642.6 11.3 %bitcast_add_fusion.2 = f32[16,256,256]{1,2,0:T(8,128)} fusion(f32[16,256,256]{1,2,0:T(8,128)} %get-tuple-element.102, f32[2,256,16,256]{3,1,0,2:T(8,128)} %fusion.29, pred[]{:T(512)S(6)} %compare.8, f32[48,256,256]{2,1,0:T(8,128)} %get-tuple-element.113, s32[]{:T(128)S(6)} %select_n.97), kind=kOutput, calls=%fused_computation.2.clone.1 | convolution fusion | flops 6444548096 | bytes 17301508 | tf_op jit(solution)/shard_map/while/body/eval_jaxpr/pac,picb->iab/dot_general | solution.py:17
  666.0 11.2 %bitcast_add_fusion.2 = f32[16,256,256]{1,2,0:T(8,128)} fusion(f32[16,256,256]{1,2,0:T(8,128)} %get-tuple-element.102, f32[2,256,16,256]{3,1,0,2:T(8,128)} %fusion.29, pred[]{:T(512)S(6)} %compare.8, f32[48,256,256]{2,1,0:T(8,128)} %get-tuple-element.113, s32[]{:T(128)S(6)} %select_n.97), kind=kOutput, calls=%fused_computation.2.clone.1 | convolution fusion | flops 6444548096 | bytes 17301508 | tf_op jit(solution)/shard_map/while/body/eval_jaxpr/pac,picb->iab/dot_general | solution.py:17
  689.3 11.2 %bitcast_add_fusion.2 = f32[16,256,256]{1,2,0:T(8,128)} fusion(f32[16,256,256]{1,2,0:T(8,128)} %get-tuple-element.102, f32[2,256,16,256]{3,1,0,2:T(8,128)} %fusion.29, pred[]{:T(512)S(6)} %compare.8, f32[48,256,256]{2,1,0:T(8,128)} %get-tuple-element.113, s32[]{:T(128)S(6)} %select_n.97), kind=kOutput, calls=%fused_computation.2.clone.1 | convolution fusion | flops 6444548096 | bytes 17301508 | tf_op jit(solution)/shard_map/while/body/eval_jaxpr/pac,picb->iab/dot_general | solution.py:17
  712.7 11.2 %bitcast_add_fusion.2 = f32[16,256,256]{1,2,0:T(8,128)} fusion(f32[16,256,256]{1,2,0:T(8,128)} %get-tuple-element.102, f32[2,256,16,256]{3,1,0,2:T(8,128)} %fusion.29, pred[]{:T(512)S(6)} %compare.8, f32[48,256,256]{2,1,0:T(8,128)} %get-tuple-element.113, s32[]{:T(128)S(6)} %select_n.97), kind=kOutput, calls=%fused_computation.2.clone.1 | convolution fusion | flops 6444548096 | bytes 17301508 | tf_op jit(solution)/shard_map/while/body/eval_jaxpr/pac,picb->iab/dot_general | solution.py:17
  736.0 11.2 %bitcast_add_fusion.2 = f32[16,256,256]{1,2,0:T(8,128)} fusion(f32[16,256,256]{1,2,0:T(8,128)} %get-tuple-element.102, f32[2,256,16,256]{3,1,0,2:T(8,128)} %fusion.29, pred[]{:T(512)S(6)} %compare.8, f32[48,256,256]{2,1,0:T(8,128)} %get-tuple-element.113, s32[]{:T(128)S(6)} %select_n.97), kind=kOutput, calls=%fused_computation.2.clone.1 | convolution fusion | flops 6444548096 | bytes 17301508 | tf_op jit(solution)/shard_map/while/body/eval_jaxpr/pac,picb->iab/dot_general | solution.py:17
  759.4 11.2 %bitcast_add_fusion.2 = f32[16,256,256]{1,2,0:T(8,128)} fusion(f32[16,256,256]{1,2,0:T(8,128)} %get-tuple-element.102, f32[2,256,16,256]{3,1,0,2:T(8,128)} %fusion.29, pred[]{:T(512)S(6)} %compare.8, f32[48,256,256]{2,1,0:T(8,128)} %get-tuple-element.113, s32[]{:T(128)S(6)} %select_n.97), kind=kOutput, calls=%fused_computation.2.clone.1 | convolution fusion | flops 6444548096 | bytes 17301508 | tf_op jit(solution)/shard_map/while/body/eval_jaxpr/pac,picb->iab/dot_general | solution.py:17
  782.8 11.2 %bitcast_add_fusion.2 = f32[16,256,256]{1,2,0:T(8,128)} fusion(f32[16,256,256]{1,2,0:T(8,128)} %get-tuple-element.102, f32[2,256,16,256]{3,1,0,2:T(8,128)} %fusion.29, pred[]{:T(512)S(6)} %compare.8, f32[48,256,256]{2,1,0:T(8,128)} %get-tuple-element.113, s32[]{:T(128)S(6)} %select_n.97), kind=kOutput, calls=%fused_computation.2.clone.1 | convolution fusion | flops 6444548096 | bytes 17301508 | tf_op jit(solution)/shard_map/while/body/eval_jaxpr/pac,picb->iab/dot_general | solution.py:17
  806.1 11.2 %bitcast_add_fusion.2 = f32[16,256,256]{1,2,0:T(8,128)} fusion(f32[16,256,256]{1,2,0:T(8,128)} %get-tuple-element.102, f32[2,256,16,256]{3,1,0,2:T(8,128)} %fusion.29, pred[]{:T(512)S(6)} %compare.8, f32[48,256,256]{2,1,0:T(8,128)} %get-tuple-element.113, s32[]{:T(128)S(6)} %select_n.97), kind=kOutput, calls=%fused_computation.2.clone.1 | convolution fusion | flops 6444548096 | bytes 17301508 | tf_op jit(solution)/shard_map/while/body/eval_jaxpr/pac,picb->iab/dot_general | solution.py:17
  825.5 17.5 %collective-permute-start.2 = (f32[8,256,256]{2,0,1:T(8,128)S(1)}, f32[8,256,256]{2,0,1:T(8,128)S(1)}, u32[]{:S(2)}, u32[]{:S(2)}) collective-permute-start(f32[8,256,256]{2,0,1:T(8,128)S(1)} %slice_select_fusion), channel_id=1, source_target_pairs={{0,4},{2,6},{4,0},{6,2},{8,12},{10,14},{12,8},{14,10},{16,20},{18,... | collective-permute-start | bytes 6291464 | tf_op jit(solution)/shard_map/ppermute | solution.py:12
  843.0 46.1 %collective-permute-done.2 = f32[8,256,256]{2,0,1:T(8,128)S(1)} collective-permute-done((f32[8,256,256]{2,0,1:T(8,128)S(1)}, f32[8,256,256]{2,0,1:T(8,128)S(1)}, u32[]{:S(2)}, u32[]{:S(2)}) %collective-permute-start.2) | collective-permute-done | bytes 2097184 | tf_op jit(solution)/shard_map/ppermute | solution.py:12
  893.8 37.8 %all-to-all-start.4 = ((f32[4,256,128]{2,0,1:T(4,128)}), f32[4,256,128]{2,0,1:T(4,128)}, u32[]{:S(2)}, u32[]{:S(2)}) async-start(f32[4,256,128]{2,0,1:T(4,128)} %bitcast.89), calls=%async_computation.4 | async-start | bytes 1048576 | tf_op jit(solution)/shard_map/all_to_all | solution.py:71
  950.1 26.1 %all-reduce.2.cloned.1.call-done = f32[4,256,256]{2,0,1:T(4,128)} async-done(((f32[4,256,256]{2,0,1:T(4,128)}), f32[4,256,256]{2,0,1:T(4,128)}) %all-reduce.2.cloned.1.call-update) | async-done | bytes 1048592 | tf_op jit(solution)/shard_map/psum | solution.py:64
  985.8 12.4 %all-to-all-done.3 = f32[4,256,128]{2,0,1:T(4,128)S(1)} async-done(((f32[4,256,128]{2,0,1:T(4,128)}), f32[4,256,128]{2,0,1:T(4,128)S(1)}, u32[]{:S(2)}, u32[]{:S(2)}) %all-to-all-start.3) | async-done | bytes 524320 | tf_op jit(solution)/shard_map/all_to_all | solution.py:69
  (100 shorter events, 374.7 us)
Async XLA Ops:
  6.5 995.9 %copy-start = (f32[192,8,8]{0,2,1:T(8,128)S(1)}, f32[192,8,8]{0,2,1:T(8,128)}, u32[]{:S(2)}) copy-start(f32[192,8,8]{0,2,1:T(8,128)} %param.7) | copy-start | bytes 147460
  14.7 7.6 copy-start.2
  14.7 231.2 %all-to-all-start = ((f32[16,48,16,256]{3,2,1,0:T(8,128)}), f32[16,48,16,256]{3,2,1,0:T(8,128)}, u32[]{:S(2)}, u32[]{:S(2)}) async-start(f32[16,48,16,256]{3,2,1,0:T(8,128)} %bitcast.83), calls=%async_computation | async-start | bytes 25165824 | tf_op jit(solution)/shard_map/all_to_all | solution.py:38
  22.4 4.0 collective-permute-start
  28.3 143.3 %collective-permute-start.1 = (f32[8,256,256]{2,1,0:T(8,128)S(1)}, f32[8,256,256]{2,1,0:T(8,128)}, u32[]{:S(2)}, u32[]{:S(2)}) collective-permute-start(f32[8,256,256]{2,1,0:T(8,128)S(1)} %maximum_select_fusion.1), channel_id=1, source_target_pairs={{0,4},{2,6},{4,0},{6,2},{8,12},{10,14},{12,8},{14,10},{16,20},{18,... | collective-permute-start | bytes 6291464 | tf_op jit(solution)/shard_map/ppermute | solution.py:12
  822.8 66.3 %copy-start.1 = (f32[16,256,256]{2,0,1:T(8,128)S(1)}, f32[16,256,256]{2,0,1:T(8,128)}, u32[]{:S(2)}) copy-start(f32[16,256,256]{2,0,1:T(8,128)} %copy.50) | copy-start | bytes 12582916
  825.5 63.7 %collective-permute-start.2 = (f32[8,256,256]{2,0,1:T(8,128)S(1)}, f32[8,256,256]{2,0,1:T(8,128)S(1)}, u32[]{:S(2)}, u32[]{:S(2)}) collective-permute-start(f32[8,256,256]{2,0,1:T(8,128)S(1)} %slice_select_fusion), channel_id=1, source_target_pairs={{0,4},{2,6},{4,0},{6,2},{8,12},{10,14},{12,8},{14,10},{16,20},{18,... | collective-permute-start | bytes 6291464 | tf_op jit(solution)/shard_map/ppermute | solution.py:12
  890.8 41.1 %collective-permute-start.3 = (f32[4,256,256]{2,0,1:T(4,128)}, f32[4,256,256]{2,0,1:T(4,128)}, u32[]{:S(2)}, u32[]{:S(2)}) collective-permute-start(f32[4,256,256]{2,0,1:T(4,128)} %slice_select_fusion.1), channel_id=1, source_target_pairs={{0,2},{2,0},{4,6},{6,4},{8,10},{10,8},{12,14},{14,12},{16,18},{18,... | collective-permute-start | bytes 3145736 | tf_op jit(solution)/shard_map/ppermute | solution.py:12
  893.8 52.1 %all-to-all-start.4 = ((f32[4,256,128]{2,0,1:T(4,128)}), f32[4,256,128]{2,0,1:T(4,128)}, u32[]{:S(2)}, u32[]{:S(2)}) async-start(f32[4,256,128]{2,0,1:T(4,128)} %bitcast.89), calls=%async_computation.4 | async-start | bytes 1048576 | tf_op jit(solution)/shard_map/all_to_all | solution.py:71
  931.6 44.6 %all-reduce.2.cloned.1.call-start = ((), (), s32[]{:S(2)}) async-start(), calls=%async_computation.5 | async-start | bytes 2097152 | tf_op jit(solution)/shard_map/psum | solution.py:64
  945.9 32.4 %all-to-all-start.2 = ((f32[4,256,128]{2,0,1:T(4,128)}), f32[4,256,128]{2,0,1:T(4,128)S(1)}, u32[]{:S(2)}, u32[]{:S(2)}) async-start(f32[4,256,128]{2,0,1:T(4,128)} %copy.68), calls=%async_computation.2 | async-start | bytes 1048576 | tf_op jit(solution)/shard_map/all_to_all | solution.py:70
  978.3 19.9 %all-to-all-start.3 = ((f32[4,256,128]{2,0,1:T(4,128)}), f32[4,256,128]{2,0,1:T(4,128)S(1)}, u32[]{:S(2)}, u32[]{:S(2)}) async-start(f32[4,256,128]{2,0,1:T(4,128)} %copy.57), calls=%async_computation.3 | async-start | bytes 1048576 | tf_op jit(solution)/shard_map/all_to_all | solution.py:69
  998.2 18.4 %all-to-all-start.1 = ((f32[4,256,128]{2,0,1:T(4,128)}), f32[4,256,128]{2,0,1:T(4,128)S(1)}, u32[]{:S(2)}, u32[]{:S(2)}) async-start(f32[4,256,128]{2,0,1:T(4,128)} %constant_dynamic-slice_fusion.2), calls=%async_computation.1 | async-start | bytes 1048576 | tf_op jit(solution)/shard_map/all_to_all | solution.py:68
Sparse Core Ops, SparseCore 0:
  934.7 41.4 all-reduce.1
where the time goes:
time: 1030 us
  matrix products  529 us (51%)
  waiting for transfers between devices  314 us (30%)
  starting transfers between devices  79.3 us (8%)
  local copies, waits for them, and re-layouts  52.8 us (5%)
  loops' own time  16.9 us (2%)
  between operations  13.6 us (1%)
  other arithmetic  13.5 us (1%)
    dot_general x24, matrix products, both_sides(): jnp.einsum('pac,picb->iab', row_block, mixed_terms, precision=highest)  269 us
    dot_general x24, matrix products, both_sides(): jnp.einsum('icd,pbd->picb', amps, row_block, precision=highest)  258 us
    ppermute x4, waiting for transfers between devices, from_partner(): return lax.ppermute(value, axis, pairs)  191 us
    all_to_all x1, waiting for transfers between devices, shards(): lax.all_to_all(outgoing, 'pairs', split_axis=0, concat_axis=2, tiled=True)  69.7 us
    all_to_all x1, starting transfers between devices, shards(): lax.all_to_all(amp_flip, 'pairs', split_axis=1, concat_axis=0, tiled=True)  37.8 us
    psum x1, waiting for transfers between devices, shards(): particle, coupling = lax.psum((particle, coupling), 'aux')  26.1 us
  transfers between devices with their start and end apart: 10, of which 8 were waited for; matrix products, arithmetic and copies ran while one was open for 2% of the time, Pallas kernels for 0%

commit v1 on v0

--- a/solution.py
+++ b/solution.py
@@ -4,6 +4,22 @@
 from jax.sharding import PartitionSpec as P
 
 highest = lax.Precision.HIGHEST
+
+
+def exchange_in_pairs(x, axis, split, join):
+    ways, here = (lax.axis_size(axis), lax.axis_index(axis))
+    width = x.shape[split] // ways
+    shape = list(x.shape)
+    shape[split] = width
+    height = shape[join]
+    shape[join] = height * ways
+    full = jnp.zeros(shape, x.dtype)
+    for mask in range(ways):
+        part = lax.dynamic_slice_in_dim(x, (here ^ mask) * width, width, axis=split)
+        if mask:
+            part = lax.ppermute(part, axis, [(d, d ^ mask) for d in range(ways)])
+        full = lax.dynamic_update_slice_in_dim(full, part, (here ^ mask) * height, axis=join)
+    return full
 
 
 def from_partner(value, axis, bit):
@@ -35,7 +51,7 @@
     outgoing = jnp.tile(quarters, (pairs_count // 4, 1, 1, 1, 1)).reshape(
         pairs_count, quarter_rows, local_rows, virt_width
     )
-    arrived = lax.all_to_all(outgoing, "pairs", split_axis=0, concat_axis=2, tiled=True)[0]
+    arrived = exchange_in_pairs(outgoing, "pairs", 0, 2)[0]
     group_amps = amplitudes
     for bit in range(2):
         mate = from_partner(group_amps, "pairs", bit)

time: 1030 us -> 1060 us (1.029)
  starting transfers between devices: 79.3 us -> 153 us
  waiting for transfers between devices: 314 us -> 250 us
  local copies, waits for them, and re-layouts: 52.8 us -> 75.4 us
    ppermute x0 -> x15, waiting for transfers between devices: none -> 150 us  [exchange_in_pairs(): part = lax.ppermute(part, axis, [(d, d ^ mask) for d in range(ways)])]
    ppermute x4, waiting for transfers between devices: 191 us -> 47.2 us  [from_partner(): return lax.ppermute(value, axis, pairs)]
    ppermute x0 -> x15, starting transfers between devices: none -> 72.1 us  [exchange_in_pairs(): part = lax.ppermute(part, axis, [(d, d ^ mask) for d in range(ways)])]
    all_to_all x1 -> x0, waiting for transfers between devices: 69.7 us -> none  [shards(): lax.all_to_all(outgoing, 'pairs', split_axis=0, concat_axis=2, tiled=True)]
    all_to_all x1, starting transfers between devices: 4.16 us -> 65.9 us  [shards(): lax.all_to_all(amp_cols, 'pairs', split_axis=1, concat_axis=0, tiled=True)]
    all_to_all x1, starting transfers between devices: 37.8 us -> 4.17 us  [shards(): lax.all_to_all(amp_flip, 'pairs', split_axis=1, concat_axis=0, tiled=True)]
    dynamic_update_slice x0 -> x16, local copies, waits for them, and re-layouts: none -> 22.1 us  [exchange_in_pairs(): lax.dynamic_update_slice_in_dim(full, part, (here ^ mask) * height, axis=...]
    ppermute x4, starting transfers between devices: 19.8 us -> 1.47 us  [from_partner(): return lax.ppermute(value, axis, pairs)]
  transfers between devices with their start and end apart: 10 -> 24, of which waited for: 8 -> 12; matrix products, arithmetic and copies ran while one was open for 2% -> 4% of each run, Pallas kernels for 0% -> 0%
where the time goes in v1:
time: 1060 us
  matrix products  532 us (50%)
  waiting for transfers between devices  250 us (24%)
  starting transfers between devices  153 us (14%)
  local copies, waits for them, and re-layouts  75.4 us (7%)
  loops' own time  16.4 us (2%)
  between operations  13.7 us (1%)
  other arithmetic  11.3 us (1%)
    dot_general x24, matrix products, both_sides(): jnp.einsum('pac,picb->iab', row_block, mixed_terms, precision=highest)  270 us
    dot_general x24, matrix products, both_sides(): jnp.einsum('icd,pbd->picb', amps, row_block, precision=highest)  260 us
    ppermute x15, waiting for transfers between devices, exchange_in_pairs(): part = lax.ppermute(part, axis, [(d, d ^ mask) for d in range(ways)])  150 us
    ppermute x15, starting transfers between devices, exchange_in_pairs(): part = lax.ppermute(part, axis, [(d, d ^ mask) for d in range(ways)])  72.1 us
    all_to_all x1, starting transfers between devices, shards(): lax.all_to_all(amp_cols, 'pairs', split_axis=1, concat_axis=0, tiled=True)  65.9 us
    ppermute x4, waiting for transfers between devices, from_partner(): return lax.ppermute(value, axis, pairs)  47.2 us
    psum x1, waiting for transfers between devices, shards(): particle, coupling = lax.psum((particle, coupling), 'aux')  26 us
    dynamic_update_slice x16, local copies, waits for them, and re-layouts, exchange_in_pairs(): lax.dynamic_update_slice_in_dim(full, part, (here ^ mask) * height, axis=...  22.1 us
  transfers between devices with their start and end apart: 24, of which 12 were waited for; matrix products, arithmetic and copies ran while one was open for 4% of the time, Pallas kernels for 0%

profile of v1, /device:TPU:0, one launch (start us, length us, event | category | flops | bytes accessed | tf_op | source)
XLA Modules:
  0.0 1060.5 jit_solution(7103931251090970261)
XLA Ops:
  48.6 12.6 %collective-permute-done.2 = f32[1,48,16,256]{3,2,1,0:T(8,128)} collective-permute-done((f32[1,48,16,256]{3,2,1,0:T(8,128)}, f32[1,48,16,256]{3,2,1,0:T(8,128)}, u32[]{:S(2)}, u32[]{:S(2)}) %collective-permute-start.2) | collective-permute-done | bytes 786464 | tf_op jit(solution)/shard_map/ppermute | solution.py:20
  70.5 44.9 %collective-permute-done.5 = f32[1,48,16,256]{3,2,1,0:T(8,128)S(1)} collective-permute-done((f32[1,48,16,256]{3,2,1,0:T(8,128)S(1)}, f32[1,48,16,256]{3,2,1,0:T(8,128)S(1)}, u32[]{:S(2)}, u32[]{:S(2)}) %collective-permute-start.5) | collective-permute-done | bytes 786464 | tf_op jit(solution)/shard_map/ppermute | solution.py:20
  116.4 14.7 %collective-permute-done.6 = f32[1,48,16,256]{3,2,1,0:T(8,128)S(1)} collective-permute-done((f32[1,48,16,256]{3,2,1,0:T(8,128)S(1)}, f32[1,48,16,256]{3,2,1,0:T(8,128)S(1)}, u32[]{:S(2)}, u32[]{:S(2)}) %collective-permute-start.6) | collective-permute-done | bytes 786464 | tf_op jit(solution)/shard_map/ppermute | solution.py:20
  135.3 51.3 %collective-permute-start.12 = (f32[1,48,16,256]{3,2,1,0:T(8,128)S(1)}, f32[1,48,16,256]{3,2,1,0:T(8,128)S(1)}, u32[]{:S(2)}, u32[]{:S(2)}) collective-permute-start(f32[1,48,16,256]{3,2,1,0:T(8,128)S(1)} %copy-done.2), channel_id=1, source_target_pairs={{0,26},{2,24},{4,30},{6,28},{8,18},{10,16},{12,22},{14,20},{16,10}... | collective-permute-start | bytes 2359304 | tf_op jit(solution)/shard_map/ppermute | solution.py:20
  187.6 30.4 %collective-permute-done.9 = f32[1,48,16,256]{3,2,1,0:T(8,128)S(1)} collective-permute-done((f32[1,48,16,256]{3,2,1,0:T(8,128)S(1)}, f32[1,48,16,256]{3,2,1,0:T(8,128)S(1)}, u32[]{:S(2)}, u32[]{:S(2)}) %collective-permute-start.9) | collective-permute-done | bytes 786464 | tf_op jit(solution)/shard_map/ppermute | solution.py:20
  222.8 28.8 %collective-permute-done.10 = f32[1,48,16,256]{3,2,1,0:T(8,128)S(1)} collective-permute-done((f32[1,48,16,256]{3,2,1,0:T(8,128)S(1)}, f32[1,48,16,256]{3,2,1,0:T(8,128)S(1)}, u32[]{:S(2)}, u32[]{:S(2)}) %collective-permute-start.10) | collective-permute-done | bytes 786464 | tf_op jit(solution)/shard_map/ppermute | solution.py:20
  258.8 15.1 %collective-permute-done.14 = f32[1,48,16,256]{3,2,1,0:T(8,128)S(1)} collective-permute-done((f32[1,48,16,256]{3,2,1,0:T(8,128)S(1)}, f32[1,48,16,256]{3,2,1,0:T(8,128)S(1)}, u32[]{:S(2)}, u32[]{:S(2)}) %collective-permute-start.14) | collective-permute-done | bytes 786464 | tf_op jit(solution)/shard_map/ppermute | solution.py:20
  277.2 562.4 %while.11 = (s32[]{:T(128)}, f32[16,256,256]{1,2,0:T(8,128)}, s32[24]{0:T(128)S(1)}, f32[48,256,256]{2,1,0:T(8,128)}, f32[16,256,256]{2,1,0:T(8,128)}, /*index=5*/s32[]{:T(128)}, s32[1]{0:T(128)}, s32[]{:T(128)}, s32[]{:T(128)}) while((s32[]{:T(128)}, f32[16,256,256]{1,2,0:T(8,128)}, s32[24]{0:T(128)S(1)}, ...), condition=%wide.region_1.2_spmd.clone, body=%wide.region_0.1_spmd.clone.sunk | while | flops 12886999040 | bytes 30408880 | solution.py:67
  312.2 11.3 %bitcast_add_fusion.2 = f32[16,256,256]{1,2,0:T(8,128)} fusion(f32[16,256,256]{1,2,0:T(8,128)} %get-tuple-element.117, f32[2,256,16,256]{3,1,0,2:T(8,128)} %fusion.29, pred[]{:T(512)S(6)} %compare.8, f32[48,256,256]{2,1,0:T(8,128)} %get-tuple-element.128, s32[]{:T(128)S(6)} %select_n.225), kind=kOutput, calls=%fused_computation.2.clone.1 | convolution fusion | flops 6444548096 | bytes 17301508 | tf_op jit(solution)/shard_map/while/body/eval_jaxpr/pac,picb->iab/dot_general | solution.py:33
  335.6 11.3 %bitcast_add_fusion.2 = f32[16,256,256]{1,2,0:T(8,128)} fusion(f32[16,256,256]{1,2,0:T(8,128)} %get-tuple-element.117, f32[2,256,16,256]{3,1,0,2:T(8,128)} %fusion.29, pred[]{:T(512)S(6)} %compare.8, f32[48,256,256]{2,1,0:T(8,128)} %get-tuple-element.128, s32[]{:T(128)S(6)} %select_n.225), kind=kOutput, calls=%fused_computation.2.clone.1 | convolution fusion | flops 6444548096 | bytes 17301508 | tf_op jit(solution)/shard_map/while/body/eval_jaxpr/pac,picb->iab/dot_general | solution.py:33
  359.1 11.3 %bitcast_add_fusion.2 = f32[16,256,256]{1,2,0:T(8,128)} fusion(f32[16,256,256]{1,2,0:T(8,128)} %get-tuple-element.117, f32[2,256,16,256]{3,1,0,2:T(8,128)} %fusion.29, pred[]{:T(512)S(6)} %compare.8, f32[48,256,256]{2,1,0:T(8,128)} %get-tuple-element.128, s32[]{:T(128)S(6)} %select_n.225), kind=kOutput, calls=%fused_computation.2.clone.1 | convolution fusion | flops 6444548096 | bytes 17301508 | tf_op jit(solution)/shard_map/while/body/eval_jaxpr/pac,picb->iab/dot_general | solution.py:33
  382.6 11.3 %bitcast_add_fusion.2 = f32[16,256,256]{1,2,0:T(8,128)} fusion(f32[16,256,256]{1,2,0:T(8,128)} %get-tuple-element.117, f32[2,256,16,256]{3,1,0,2:T(8,128)} %fusion.29, pred[]{:T(512)S(6)} %compare.8, f32[48,256,256]{2,1,0:T(8,128)} %get-tuple-element.128, s32[]{:T(128)S(6)} %select_n.225), kind=kOutput, calls=%fused_computation.2.clone.1 | convolution fusion | flops 6444548096 | bytes 17301508 | tf_op jit(solution)/shard_map/while/body/eval_jaxpr/pac,picb->iab/dot_general | solution.py:33
  406.0 11.3 %bitcast_add_fusion.2 = f32[16,256,256]{1,2,0:T(8,128)} fusion(f32[16,256,256]{1,2,0:T(8,128)} %get-tuple-element.117, f32[2,256,16,256]{3,1,0,2:T(8,128)} %fusion.29, pred[]{:T(512)S(6)} %compare.8, f32[48,256,256]{2,1,0:T(8,128)} %get-tuple-element.128, s32[]{:T(128)S(6)} %select_n.225), kind=kOutput, calls=%fused_computation.2.clone.1 | convolution fusion | flops 6444548096 | bytes 17301508 | tf_op jit(solution)/shard_map/while/body/eval_jaxpr/pac,picb->iab/dot_general | solution.py:33
  429.5 11.3 %bitcast_add_fusion.2 = f32[16,256,256]{1,2,0:T(8,128)} fusion(f32[16,256,256]{1,2,0:T(8,128)} %get-tuple-element.117, f32[2,256,16,256]{3,1,0,2:T(8,128)} %fusion.29, pred[]{:T(512)S(6)} %compare.8, f32[48,256,256]{2,1,0:T(8,128)} %get-tuple-element.128, s32[]{:T(128)S(6)} %select_n.225), kind=kOutput, calls=%fused_computation.2.clone.1 | convolution fusion | flops 6444548096 | bytes 17301508 | tf_op jit(solution)/shard_map/while/body/eval_jaxpr/pac,picb->iab/dot_general | solution.py:33
  452.9 11.3 %bitcast_add_fusion.2 = f32[16,256,256]{1,2,0:T(8,128)} fusion(f32[16,256,256]{1,2,0:T(8,128)} %get-tuple-element.117, f32[2,256,16,256]{3,1,0,2:T(8,128)} %fusion.29, pred[]{:T(512)S(6)} %compare.8, f32[48,256,256]{2,1,0:T(8,128)} %get-tuple-element.128, s32[]{:T(128)S(6)} %select_n.225), kind=kOutput, calls=%fused_computation.2.clone.1 | convolution fusion | flops 6444548096 | bytes 17301508 | tf_op jit(solution)/shard_map/while/body/eval_jaxpr/pac,picb->iab/dot_general | solution.py:33
  476.4 11.3 %bitcast_add_fusion.2 = f32[16,256,256]{1,2,0:T(8,128)} fusion(f32[16,256,256]{1,2,0:T(8,128)} %get-tuple-element.117, f32[2,256,16,256]{3,1,0,2:T(8,128)} %fusion.29, pred[]{:T(512)S(6)} %compare.8, f32[48,256,256]{2,1,0:T(8,128)} %get-tuple-element.128, s32[]{:T(128)S(6)} %select_n.225), kind=kOutput, calls=%fused_computation.2.clone.1 | convolution fusion | flops 6444548096 | bytes 17301508 | tf_op jit(solution)/shard_map/while/body/eval_jaxpr/pac,picb->iab/dot_general | solution.py:33
  523.3 11.3 %bitcast_add_fusion.2 = f32[16,256,256]{1,2,0:T(8,128)} fusion(f32[16,256,256]{1,2,0:T(8,128)} %get-tuple-element.117, f32[2,256,16,256]{3,1,0,2:T(8,128)} %fusion.29, pred[]{:T(512)S(6)} %compare.8, f32[48,256,256]{2,1,0:T(8,128)} %get-tuple-element.128, s32[]{:T(128)S(6)} %select_n.225), kind=kOutput, calls=%fused_computation.2.clone.1 | convolution fusion | flops 6444548096 | bytes 17301508 | tf_op jit(solution)/shard_map/while/body/eval_jaxpr/pac,picb->iab/dot_general | solution.py:33
  546.8 11.3 %bitcast_add_fusion.2 = f32[16,256,256]{1,2,0:T(8,128)} fusion(f32[16,256,256]{1,2,0:T(8,128)} %get-tuple-element.117, f32[2,256,16,256]{3,1,0,2:T(8,128)} %fusion.29, pred[]{:T(512)S(6)} %compare.8, f32[48,256,256]{2,1,0:T(8,128)} %get-tuple-element.128, s32[]{:T(128)S(6)} %select_n.225), kind=kOutput, calls=%fused_computation.2.clone.1 | convolution fusion | flops 6444548096 | bytes 17301508 | tf_op jit(solution)/shard_map/while/body/eval_jaxpr/pac,picb->iab/dot_general | solution.py:33
  570.2 11.3 %bitcast_add_fusion.2 = f32[16,256,256]{1,2,0:T(8,128)} fusion(f32[16,256,256]{1,2,0:T(8,128)} %get-tuple-element.117, f32[2,256,16,256]{3,1,0,2:T(8,128)} %fusion.29, pred[]{:T(512)S(6)} %compare.8, f32[48,256,256]{2,1,0:T(8,128)} %get-tuple-element.128, s32[]{:T(128)S(6)} %select_n.225), kind=kOutput, calls=%fused_computation.2.clone.1 | convolution fusion | flops 6444548096 | bytes 17301508 | tf_op jit(solution)/shard_map/while/body/eval_jaxpr/pac,picb->iab/dot_general | solution.py:33
  593.7 11.3 %bitcast_add_fusion.2 = f32[16,256,256]{1,2,0:T(8,128)} fusion(f32[16,256,256]{1,2,0:T(8,128)} %get-tuple-element.117, f32[2,256,16,256]{3,1,0,2:T(8,128)} %fusion.29, pred[]{:T(512)S(6)} %compare.8, f32[48,256,256]{2,1,0:T(8,128)} %get-tuple-element.128, s32[]{:T(128)S(6)} %select_n.225), kind=kOutput, calls=%fused_computation.2.clone.1 | convolution fusion | flops 6444548096 | bytes 17301508 | tf_op jit(solution)/shard_map/while/body/eval_jaxpr/pac,picb->iab/dot_general | solution.py:33
  617.1 11.3 %bitcast_add_fusion.2 = f32[16,256,256]{1,2,0:T(8,128)} fusion(f32[16,256,256]{1,2,0:T(8,128)} %get-tuple-element.117, f32[2,256,16,256]{3,1,0,2:T(8,128)} %fusion.29, pred[]{:T(512)S(6)} %compare.8, f32[48,256,256]{2,1,0:T(8,128)} %get-tuple-element.128, s32[]{:T(128)S(6)} %select_n.225), kind=kOutput, calls=%fused_computation.2.clone.1 | convolution fusion | flops 6444548096 | bytes 17301508 | tf_op jit(solution)/shard_map/while/body/eval_jaxpr/pac,picb->iab/dot_general | solution.py:33
  640.6 11.3 %bitcast_add_fusion.2 = f32[16,256,256]{1,2,0:T(8,128)} fusion(f32[16,256,256]{1,2,0:T(8,128)} %get-tuple-element.117, f32[2,256,16,256]{3,1,0,2:T(8,128)} %fusion.29, pred[]{:T(512)S(6)} %compare.8, f32[48,256,256]{2,1,0:T(8,128)} %get-tuple-element.128, s32[]{:T(128)S(6)} %select_n.225), kind=kOutput, calls=%fused_computation.2.clone.1 | convolution fusion | flops 6444548096 | bytes 17301508 | tf_op jit(solution)/shard_map/while/body/eval_jaxpr/pac,picb->iab/dot_general | solution.py:33
  664.0 11.3 %bitcast_add_fusion.2 = f32[16,256,256]{1,2,0:T(8,128)} fusion(f32[16,256,256]{1,2,0:T(8,128)} %get-tuple-element.117, f32[2,256,16,256]{3,1,0,2:T(8,128)} %fusion.29, pred[]{:T(512)S(6)} %compare.8, f32[48,256,256]{2,1,0:T(8,128)} %get-tuple-element.128, s32[]{:T(128)S(6)} %select_n.225), kind=kOutput, calls=%fused_computation.2.clone.1 | convolution fusion | flops 6444548096 | bytes 17301508 | tf_op jit(solution)/shard_map/while/body/eval_jaxpr/pac,picb->iab/dot_general | solution.py:33
  687.5 11.3 %bitcast_add_fusion.2 = f32[16,256,256]{1,2,0:T(8,128)} fusion(f32[16,256,256]{1,2,0:T(8,128)} %get-tuple-element.117, f32[2,256,16,256]{3,1,0,2:T(8,128)} %fusion.29, pred[]{:T(512)S(6)} %compare.8, f32[48,256,256]{2,1,0:T(8,128)} %get-tuple-element.128, s32[]{:T(128)S(6)} %select_n.225), kind=kOutput, calls=%fused_computation.2.clone.1 | convolution fusion | flops 6444548096 | bytes 17301508 | tf_op jit(solution)/shard_map/while/body/eval_jaxpr/pac,picb->iab/dot_general | solution.py:33
  711.0 11.3 %bitcast_add_fusion.2 = f32[16,256,256]{1,2,0:T(8,128)} fusion(f32[16,256,256]{1,2,0:T(8,128)} %get-tuple-element.117, f32[2,256,16,256]{3,1,0,2:T(8,128)} %fusion.29, pred[]{:T(512)S(6)} %compare.8, f32[48,256,256]{2,1,0:T(8,128)} %get-tuple-element.128, s32[]{:T(128)S(6)} %select_n.225), kind=kOutput, calls=%fused_computation.2.clone.1 | convolution fusion | flops 6444548096 | bytes 17301508 | tf_op jit(solution)/shard_map/while/body/eval_jaxpr/pac,picb->iab/dot_general | solution.py:33
  734.4 11.3 %bitcast_add_fusion.2 = f32[16,256,256]{1,2,0:T(8,128)} fusion(f32[16,256,256]{1,2,0:T(8,128)} %get-tuple-element.117, f32[2,256,16,256]{3,1,0,2:T(8,128)} %fusion.29, pred[]{:T(512)S(6)} %compare.8, f32[48,256,256]{2,1,0:T(8,128)} %get-tuple-element.128, s32[]{:T(128)S(6)} %select_n.225), kind=kOutput, calls=%fused_computation.2.clone.1 | convolution fusion | flops 6444548096 | bytes 17301508 | tf_op jit(solution)/shard_map/while/body/eval_jaxpr/pac,picb->iab/dot_general | solution.py:33
  757.9 11.3 %bitcast_add_fusion.2 = f32[16,256,256]{1,2,0:T(8,128)} fusion(f32[16,256,256]{1,2,0:T(8,128)} %get-tuple-element.117, f32[2,256,16,256]{3,1,0,2:T(8,128)} %fusion.29, pred[]{:T(512)S(6)} %compare.8, f32[48,256,256]{2,1,0:T(8,128)} %get-tuple-element.128, s32[]{:T(128)S(6)} %select_n.225), kind=kOutput, calls=%fused_computation.2.clone.1 | convolution fusion | flops 6444548096 | bytes 17301508 | tf_op jit(solution)/shard_map/while/body/eval_jaxpr/pac,picb->iab/dot_general | solution.py:33
  804.8 11.3 %bitcast_add_fusion.2 = f32[16,256,256]{1,2,0:T(8,128)} fusion(f32[16,256,256]{1,2,0:T(8,128)} %get-tuple-element.117, f32[2,256,16,256]{3,1,0,2:T(8,128)} %fusion.29, pred[]{:T(512)S(6)} %compare.8, f32[48,256,256]{2,1,0:T(8,128)} %get-tuple-element.128, s32[]{:T(128)S(6)} %select_n.225), kind=kOutput, calls=%fused_computation.2.clone.1 | convolution fusion | flops 6444548096 | bytes 17301508 | tf_op jit(solution)/shard_map/while/body/eval_jaxpr/pac,picb->iab/dot_general | solution.py:33
  848.1 47.2 %collective-permute-done.17 = f32[8,256,256]{2,0,1:T(8,128)S(1)} collective-permute-done((f32[8,256,256]{2,0,1:T(8,128)S(1)}, f32[8,256,256]{2,0,1:T(8,128)S(1)}, u32[]{:S(2)}, u32[]{:S(2)}) %collective-permute-start.17) | collective-permute-done | bytes 2097184 | tf_op jit(solution)/shard_map/ppermute | solution.py:28
  900.3 65.9 %all-to-all-start.1 = ((f32[4,256,128]{2,0,1:T(4,128)}), f32[4,256,128]{2,0,1:T(4,128)}, u32[]{:S(2)}, u32[]{:S(2)}) async-start(f32[4,256,128]{2,0,1:T(4,128)} %copy.49), calls=%async_computation.1 | async-start | bytes 1048576 | tf_op jit(solution)/shard_map/all_to_all | solution.py:86
  984.7 26.0 %all-reduce.2.cloned.1.call-done = f32[4,256,256]{2,0,1:T(4,128)} async-done(((f32[4,256,256]{2,0,1:T(4,128)}), f32[4,256,256]{2,0,1:T(4,128)}) %all-reduce.2.cloned.1.call-update) | async-done | bytes 1048592 | tf_op jit(solution)/shard_map/psum | solution.py:80
  1020.3 12.1 %all-to-all-done = f32[4,256,128]{2,0,1:T(4,128)S(1)} async-done(((f32[4,256,128]{2,0,1:T(4,128)}), f32[4,256,128]{2,0,1:T(4,128)S(1)}, u32[]{:S(2)}, u32[]{:S(2)}) %all-to-all-start) | async-done | bytes 524320 | tf_op jit(solution)/shard_map/all_to_all | solution.py:84
  (159 shorter events, 455.4 us)
Async XLA Ops:
  6.5 1030.1 %copy-start = (f32[192,8,8]{0,2,1:T(8,128)S(1)}, f32[192,8,8]{0,2,1:T(8,128)}, u32[]{:S(2)}) copy-start(f32[192,8,8]{0,2,1:T(8,128)} %param.7) | copy-start | bytes 147460
  23.0 42.8 %copy-start.1 = (f32[4,256,256]{2,1,0:T(8,128)S(1)}, f32[4,256,256]{2,1,0:T(8,128)}, u32[]{:S(2)}) copy-start(f32[4,256,256]{2,1,0:T(8,128)} %param.5) | copy-start | bytes 3145732
  23.0 13.2 %collective-permute-start = (f32[1,48,16,256]{3,2,1,0:T(8,128)}, f32[1,48,16,256]{3,2,1,0:T(8,128)}, u32[]{:S(2)}, u32[]{:S(2)}) collective-permute-start(f32[1,48,16,256]{3,2,1,0:T(8,128)} %get-tuple-element.75), channel_id=1, source_target_pairs={{0,2},{2,0},{4,6},{6,4},{8,10},{10,8},{12,14},{14,12},{16,18},{18,... | collective-permute-start | bytes 2359304 | tf_op jit(solution)/shard_map/ppermute | solution.py:20
  23.6 21.3 %collective-permute-start.1 = (f32[1,48,16,256]{3,2,1,0:T(8,128)}, f32[1,48,16,256]{3,2,1,0:T(8,128)}, u32[]{:S(2)}, u32[]{:S(2)}) collective-permute-start(f32[1,48,16,256]{3,2,1,0:T(8,128)} %get-tuple-element.74), channel_id=1, source_target_pairs={{0,4},{2,6},{4,0},{6,2},{8,12},{10,14},{12,8},{14,10},{16,20},{18,... | collective-permute-start | bytes 2359304 | tf_op jit(solution)/shard_map/ppermute | solution.py:20
  26.1 35.0 %collective-permute-start.2 = (f32[1,48,16,256]{3,2,1,0:T(8,128)}, f32[1,48,16,256]{3,2,1,0:T(8,128)}, u32[]{:S(2)}, u32[]{:S(2)}) collective-permute-start(f32[1,48,16,256]{3,2,1,0:T(8,128)} %get-tuple-element.73), channel_id=1, source_target_pairs={{0,6},{2,4},{4,2},{6,0},{8,14},{10,12},{12,10},{14,8},{16,22},{18,... | collective-permute-start | bytes 2359304 | tf_op jit(solution)/shard_map/ppermute | solution.py:20
  26.2 39.6 %collective-permute-start.3 = (f32[1,48,16,256]{3,2,1,0:T(8,128)}, f32[1,48,16,256]{3,2,1,0:T(8,128)}, u32[]{:S(2)}, u32[]{:S(2)}) collective-permute-start(f32[1,48,16,256]{3,2,1,0:T(8,128)} %get-tuple-element.72), channel_id=1, source_target_pairs={{0,8},{2,10},{4,12},{6,14},{8,0},{10,2},{12,4},{14,6},{16,24},{18,... | collective-permute-start | bytes 2359304 | tf_op jit(solution)/shard_map/ppermute | solution.py:20
  28.0 40.3 %collective-permute-start.4 = (f32[1,48,16,256]{3,2,1,0:T(8,128)}, f32[1,48,16,256]{3,2,1,0:T(8,128)}, u32[]{:S(2)}, u32[]{:S(2)}) collective-permute-start(f32[1,48,16,256]{3,2,1,0:T(8,128)} %get-tuple-element.71), channel_id=1, source_target_pairs={{0,10},{2,8},{4,14},{6,12},{8,2},{10,0},{12,6},{14,4},{16,26},{18,... | collective-permute-start | bytes 2359304 | tf_op jit(solution)/shard_map/ppermute | solution.py:20
  28.0 33.2 %copy-start.7 = (f32[1,48,16,256]{3,2,1,0:T(8,128)S(1)}, f32[1,48,16,256]{3,2,1,0:T(8,128)}, u32[]{:S(2)}) copy-start(f32[1,48,16,256]{3,2,1,0:T(8,128)} %get-tuple-element.68) | copy-start | bytes 2359300
  28.0 40.3 %copy-start.6 = (f32[1,48,16,256]{3,2,1,0:T(8,128)S(1)}, f32[1,48,16,256]{3,2,1,0:T(8,128)}, u32[]{:S(2)}) copy-start(f32[1,48,16,256]{3,2,1,0:T(8,128)} %get-tuple-element.67) | copy-start | bytes 2359300
  28.0 87.4 %copy-start.5 = (f32[1,48,16,256]{3,2,1,0:T(8,128)S(1)}, f32[1,48,16,256]{3,2,1,0:T(8,128)}, u32[]{:S(2)}) copy-start(f32[1,48,16,256]{3,2,1,0:T(8,128)} %get-tuple-element.66) | copy-start | bytes 2359300
  28.0 103.1 %copy-start.4 = (f32[1,48,16,256]{3,2,1,0:T(8,128)S(1)}, f32[1,48,16,256]{3,2,1,0:T(8,128)}, u32[]{:S(2)}) copy-start(f32[1,48,16,256]{3,2,1,0:T(8,128)} %get-tuple-element.65) | copy-start | bytes 2359300
  28.0 104.0 %copy-start.3 = (f32[1,48,16,256]{3,2,1,0:T(8,128)S(1)}, f32[1,48,16,256]{3,2,1,0:T(8,128)}, u32[]{:S(2)}) copy-start(f32[1,48,16,256]{3,2,1,0:T(8,128)} %get-tuple-element.64) | copy-start | bytes 2359300
  28.0 107.3 %copy-start.2 = (f32[1,48,16,256]{3,2,1,0:T(8,128)S(1)}, f32[1,48,16,256]{3,2,1,0:T(8,128)}, u32[]{:S(2)}) copy-start(f32[1,48,16,256]{3,2,1,0:T(8,128)} %get-tuple-element.63) | copy-start | bytes 2359300
  36.2 79.2 %collective-permute-start.5 = (f32[1,48,16,256]{3,2,1,0:T(8,128)S(1)}, f32[1,48,16,256]{3,2,1,0:T(8,128)S(1)}, u32[]{:S(2)}, u32[]{:S(2)}) collective-permute-start(f32[1,48,16,256]{3,2,1,0:T(8,128)S(1)} %copy-done.9), channel_id=1, source_target_pairs={{0,12},{2,14},{4,8},{6,10},{8,4},{10,6},{12,0},{14,2},{16,28},{18,... | collective-permute-start | bytes 2359304 | tf_op jit(solution)/shard_map/ppermute | solution.py:20
  44.9 86.2 %collective-permute-start.6 = (f32[1,48,16,256]{3,2,1,0:T(8,128)S(1)}, f32[1,48,16,256]{3,2,1,0:T(8,128)S(1)}, u32[]{:S(2)}, u32[]{:S(2)}) collective-permute-start(f32[1,48,16,256]{3,2,1,0:T(8,128)S(1)} %copy-done.8), channel_id=1, source_target_pairs={{0,14},{2,12},{4,10},{6,8},{8,6},{10,4},{12,2},{14,0},{16,30},{18,... | collective-permute-start | bytes 2359304 | tf_op jit(solution)/shard_map/ppermute | solution.py:20
  61.2 72.7 %collective-permute-start.7 = (f32[1,48,16,256]{3,2,1,0:T(8,128)S(1)}, f32[1,48,16,256]{3,2,1,0:T(8,128)S(1)}, u32[]{:S(2)}, u32[]{:S(2)}) collective-permute-start(f32[1,48,16,256]{3,2,1,0:T(8,128)S(1)} %copy-done.7), channel_id=1, source_target_pairs={{0,16},{2,18},{4,20},{6,22},{8,24},{10,26},{12,28},{14,30},{16,0},... | collective-permute-start | bytes 2359304 | tf_op jit(solution)/shard_map/ppermute | solution.py:20
  65.8 66.3 %collective-permute-start.15 = (f32[4,256,256]{2,1,0:T(8,128)S(1)}, f32[4,256,256]{2,1,0:T(8,128)S(1)}, u32[]{:S(2)}, u32[]{:S(2)}) collective-permute-start(f32[4,256,256]{2,1,0:T(8,128)S(1)} %copy-done.1), channel_id=1, source_target_pairs={{0,2},{2,0},{4,6},{6,4},{8,10},{10,8},{12,14},{14,12},{16,18},{18,... | collective-permute-start | bytes 3145736 | tf_op jit(solution)/shard_map/ppermute | solution.py:28
  68.3 67.1 %collective-permute-start.8 = (f32[1,48,16,256]{3,2,1,0:T(8,128)S(1)}, f32[1,48,16,256]{3,2,1,0:T(8,128)S(1)}, u32[]{:S(2)}, u32[]{:S(2)}) collective-permute-start(f32[1,48,16,256]{3,2,1,0:T(8,128)S(1)} %copy-done.6), channel_id=1, source_target_pairs={{0,18},{2,16},{4,22},{6,20},{8,26},{10,24},{12,30},{14,28},{16,2},... | collective-permute-start | bytes 2359304 | tf_op jit(solution)/shard_map/ppermute | solution.py:20
  115.4 102.6 %collective-permute-start.9 = (f32[1,48,16,256]{3,2,1,0:T(8,128)S(1)}, f32[1,48,16,256]{3,2,1,0:T(8,128)S(1)}, u32[]{:S(2)}, u32[]{:S(2)}) collective-permute-start(f32[1,48,16,256]{3,2,1,0:T(8,128)S(1)} %copy-done.5), channel_id=1, source_target_pairs={{0,20},{2,22},{4,16},{6,18},{8,28},{10,30},{12,24},{14,26},{16,4},... | collective-permute-start | bytes 2359304 | tf_op jit(solution)/shard_map/ppermute | solution.py:20
  131.1 120.5 %collective-permute-start.10 = (f32[1,48,16,256]{3,2,1,0:T(8,128)S(1)}, f32[1,48,16,256]{3,2,1,0:T(8,128)S(1)}, u32[]{:S(2)}, u32[]{:S(2)}) collective-permute-start(f32[1,48,16,256]{3,2,1,0:T(8,128)S(1)} %copy-done.4), channel_id=1, source_target_pairs={{0,22},{2,20},{4,18},{6,16},{8,30},{10,28},{12,26},{14,24},{16,6},... | collective-permute-start | bytes 2359304 | tf_op jit(solution)/shard_map/ppermute | solution.py:20
  132.1 123.8 %collective-permute-start.11 = (f32[1,48,16,256]{3,2,1,0:T(8,128)S(1)}, f32[1,48,16,256]{3,2,1,0:T(8,128)S(1)}, u32[]{:S(2)}, u32[]{:S(2)}) collective-permute-start(f32[1,48,16,256]{3,2,1,0:T(8,128)S(1)} %copy-done.3), channel_id=1, source_target_pairs={{0,24},{2,26},{4,28},{6,30},{8,16},{10,18},{12,20},{14,22},{16,8},... | collective-permute-start | bytes 2359304 | tf_op jit(solution)/shard_map/ppermute | solution.py:20
  133.9 141.0 %collective-permute-start.16 = (f32[8,256,256]{2,1,0:T(8,128)S(1)}, f32[8,256,256]{2,1,0:T(8,128)S(1)}, u32[]{:S(2)}, u32[]{:S(2)}) collective-permute-start(f32[8,256,256]{2,1,0:T(8,128)S(1)} %maximum_select_fusion.1), channel_id=1, source_target_pairs={{0,4},{2,6},{4,0},{6,2},{8,12},{10,14},{12,8},{14,10},{16,20},{18,... | collective-permute-start | bytes 6291464 | tf_op jit(solution)/shard_map/ppermute | solution.py:28
  135.3 121.5 %collective-permute-start.12 = (f32[1,48,16,256]{3,2,1,0:T(8,128)S(1)}, f32[1,48,16,256]{3,2,1,0:T(8,128)S(1)}, u32[]{:S(2)}, u32[]{:S(2)}) collective-permute-start(f32[1,48,16,256]{3,2,1,0:T(8,128)S(1)} %copy-done.2), channel_id=1, source_target_pairs={{0,26},{2,24},{4,30},{6,28},{8,18},{10,16},{12,22},{14,20},{16,10}... | collective-permute-start | bytes 2359304 | tf_op jit(solution)/shard_map/ppermute | solution.py:20
  218.0 39.8 %collective-permute-start.13 = (f32[1,48,16,256]{3,2,1,0:T(8,128)S(1)}, f32[1,48,16,256]{3,2,1,0:T(8,128)S(1)}, u32[]{:S(2)}, u32[]{:S(2)}) collective-permute-start(f32[1,48,16,256]{3,2,1,0:T(8,128)S(1)} %get-tuple-element.62), channel_id=1, source_target_pairs={{0,28},{2,30},{4,24},{6,26},{8,20},{10,22},{12,16},{14,18},{16,12}... | collective-permute-start | bytes 2359304 | tf_op jit(solution)/shard_map/ppermute | solution.py:20
  251.6 22.3 %collective-permute-start.14 = (f32[1,48,16,256]{3,2,1,0:T(8,128)S(1)}, f32[1,48,16,256]{3,2,1,0:T(8,128)S(1)}, u32[]{:S(2)}, u32[]{:S(2)}) collective-permute-start(f32[1,48,16,256]{3,2,1,0:T(8,128)S(1)} %get-tuple-element.61), channel_id=1, source_target_pairs={{0,30},{2,28},{4,26},{6,24},{8,22},{10,20},{12,18},{14,16},{16,14}... | collective-permute-start | bytes 2359304 | tf_op jit(solution)/shard_map/ppermute | solution.py:20
  847.5 47.7 %collective-permute-start.17 = (f32[8,256,256]{2,0,1:T(8,128)S(1)}, f32[8,256,256]{2,0,1:T(8,128)S(1)}, u32[]{:S(2)}, u32[]{:S(2)}) collective-permute-start(f32[8,256,256]{2,0,1:T(8,128)S(1)} %slice_select_fusion), channel_id=1, source_target_pairs={{0,4},{2,6},{4,0},{6,2},{8,12},{10,14},{12,8},{14,10},{16,20},{18,... | collective-permute-start | bytes 6291464 | tf_op jit(solution)/shard_map/ppermute | solution.py:28
  899.1 67.2 %collective-permute-start.18 = (f32[4,256,256]{2,0,1:T(4,128)}, f32[4,256,256]{2,0,1:T(4,128)}, u32[]{:S(2)}, u32[]{:S(2)}) collective-permute-start(f32[4,256,256]{2,0,1:T(4,128)} %slice_select_fusion.1), channel_id=1, source_target_pairs={{0,2},{2,0},{4,6},{6,4},{8,10},{10,8},{12,14},{14,12},{16,18},{18,... | collective-permute-start | bytes 3145736 | tf_op jit(solution)/shard_map/ppermute | solution.py:28
  900.3 80.3 %all-to-all-start.1 = ((f32[4,256,128]{2,0,1:T(4,128)}), f32[4,256,128]{2,0,1:T(4,128)}, u32[]{:S(2)}, u32[]{:S(2)}) async-start(f32[4,256,128]{2,0,1:T(4,128)} %copy.49), calls=%async_computation.1 | async-start | bytes 1048576 | tf_op jit(solution)/shard_map/all_to_all | solution.py:86
  966.2 44.5 %all-reduce.2.cloned.1.call-start = ((), (), s32[]{:S(2)}) async-start(), calls=%async_computation.4 | async-start | bytes 2097152 | tf_op jit(solution)/shard_map/psum | solution.py:80
  980.5 32.0 %all-to-all-start.3 = ((f32[4,256,128]{2,0,1:T(4,128)}), f32[4,256,128]{2,0,1:T(4,128)S(1)}, u32[]{:S(2)}, u32[]{:S(2)}) async-start(f32[4,256,128]{2,0,1:T(4,128)} %bitcast.32), calls=%async_computation.3 | async-start | bytes 1048576 | tf_op jit(solution)/shard_map/all_to_all | solution.py:87
  1012.5 19.9 %all-to-all-start = ((f32[4,256,128]{2,0,1:T(4,128)}), f32[4,256,128]{2,0,1:T(4,128)S(1)}, u32[]{:S(2)}, u32[]{:S(2)}) async-start(f32[4,256,128]{2,0,1:T(4,128)} %constant_dynamic-slice_fusion.1), calls=%async_computation | async-start | bytes 1048576 | tf_op jit(solution)/shard_map/all_to_all | solution.py:84
  1032.4 18.4 %all-to-all-start.2 = ((f32[4,256,128]{2,0,1:T(4,128)}), f32[4,256,128]{2,0,1:T(4,128)S(1)}, u32[]{:S(2)}, u32[]{:S(2)}) async-start(f32[4,256,128]{2,0,1:T(4,128)} %copy.38), calls=%async_computation.2 | async-start | bytes 1048576 | tf_op jit(solution)/shard_map/all_to_all | solution.py:85
  (2 other events, 25.1 us)
Sparse Core Ops, SparseCore 0:
  969.3 41.3 all-reduce.1
